TPU v7x, 128 devices: a whole 4x4x4 slice. The times are simulated.
128 devices in a mesh: item: 4 (over z), user: 32 (over y, x, core).
Axes of the slice: x: 4, y: 4, z: 4, core: 2. Of those that a mesh axis runs over, the one named last changes fastest.
Arguments:
- interactions: bfloat16 [65536, 16384], P('user', 'item'), may hold values from 0 to 1, as said below
- omega: float32 [16384, 256], P('item'), may hold values from -6 to 6
Outputs:
- scaled_basis: float32 [16384, 256], P('item')
Inputs may be any that keep to these rules, and one draw needn't show every extreme that they name: `interactions`: every entry is 0 or 1.
All inputs are finite; a program needn't handle non-finite values.
Results may differ from a plain program's by a relative error of at most 0.0003.
Values sent between devices are 32-bit elements; how exact they have to be, the bound alone decides.
No kernel may reach another device: no remote copies, remote signals or barrier semaphores. Data moves between devices by JAX's collectives and lax.ppermute only.
A program may use at most 128 MiB of HBM per device.

v0:
```python
import jax
import jax.numpy as jnp
from jax import lax
from jax.sharding import PartitionSpec as P

ridge = 200.0
highest = lax.Precision.HIGHEST


def gram_of(block):
    return lax.dot_general(
        block,
        block,
        (((0,), (0,)), ((), ())),
        precision=highest,
        preferred_element_type=jnp.float32,
    )


def factor(block, gram):
    lower = jnp.linalg.cholesky(gram)
    return lax.linalg.triangular_solve(lower, block, left_side=False, lower=True, transpose_a=True)


def gram_wide(block):
    return lax.psum(gram_of(block), ("item", "user"))


def local(interactions, omega):
    local_rows = jnp.dot(interactions, omega, precision=highest, preferred_element_type=jnp.float32)
    user_sketch = lax.psum(local_rows, "item")
    item_count = omega.shape[0] * lax.axis_size("item")
    factor_scale = jnp.sqrt(jnp.float32(item_count))
    own_rows = omega.shape[0] // lax.axis_size("user")
    block = lax.psum_scatter(
        lax.dot_general(
            interactions,
            user_sketch,
            (((0,), (0,)), ((), ())),
            precision=highest,
            preferred_element_type=jnp.float32,
        ),
        "user",
        scatter_dimension=0,
        tiled=True,
    )
    own_omega = lax.dynamic_slice_in_dim(omega, lax.axis_index("user") * own_rows, own_rows, 0)
    block = block + ridge * own_omega
    for sweep in range(2):
        block = factor(block, gram_wide(block))
    return lax.all_gather(factor_scale * block, "user", axis=0, tiled=True)


def solution(mesh):
    in_specs = (P("user", "item"), P("item", None))
    out_specs = P("item", None)
    return jax.shard_map(local, mesh=mesh, in_specs=in_specs, out_specs=out_specs, check_vma=False)
```

profile of v0, /device:TPU:1, one launch (start us, length us, event | category | flops | bytes accessed | tf_op | source)
XLA Modules:
  0.0 661.8 jit_solution(2004291830693291663)
XLA Ops:
  6.5 18.5 %fusion.27 = f32[2048,256]{1,0:T(8,128)} fusion(bf16[2048,4096]{1,0:T(8,128)(2,1)} %param.5, f32[4096,256]{1,0:T(8,128)} %param.6), kind=kOutput, calls=%fused_computation.63 | convolution fusion | flops 25769803776 | bytes 23068672 | tf_op jit(solution)/shard_map/dot_general | solution.py:30
  25.1 62.1 %all-reduce.5.cloned.1.call-done = f32[2048,256]{1,0:T(8,128)} async-done(((f32[2048,256]{1,0:T(8,128)}), f32[2048,256]{1,0:T(8,128)}) %all-reduce.5.cloned.1.call-update) | async-done | bytes 2097168 | tf_op jit(solution)/shard_map/psum | solution.py:31
  87.2 17.8 %convolution_bitcast_fusion = f32[4096,256]{0,1:T(8,128)} fusion(f32[2048,256]{1,0:T(8,128)} %all-reduce.5.cloned.1.call-done, bf16[2048,4096]{1,0:T(8,128)(2,1)} %param.5), kind=kOutput, calls=%fused_computation.4 | convolution fusion | flops 25769803776 | bytes 23068672 | tf_op jit(solution)/shard_map/dot_general | solution.py:36
  106.1 79.4 %reduce-scatter.2.cloned.1.call-done = f32[128,256]{0,1:T(8,128)} async-done(((f32[4096,256]{0,1:T(8,128)}), f32[128,256]{0,1:T(8,128)}) %reduce-scatter.2.cloned.1.call-update) | async-done | bytes 131088 | tf_op jit(solution)/shard_map/reduce_scatter | solution.py:35
  186.4 1.1 fusion.28
  187.8 146.7 %all-reduce.7.cloned.1.call-done = f32[256,256]{0,1:T(8,128)} async-done(((f32[256,256]{0,1:T(8,128)}), f32[256,256]{0,1:T(8,128)}) %all-reduce.7.cloned.1.call-update) | async-done | bytes 262160 | tf_op jit(solution)/shard_map/psum | solution.py:26
  336.6 11.7 %cholesky.130 = f32[128,128]{1,0:T(8,128)S(1)} custom-call(f32[128,128]{1,0:T(8,128)S(1)} %cholesky.194), custom_call_target="Cholesky" | custom-call | tf_op jit(solution)/shard_map/jit(cholesky)/cholesky | solution.py:21
  348.3 9.8 %custom-call.13 = f32[1,128,128]{1,2,0:T(8,128)S(1)} custom-call(f32[1,128,128]{2,1,0:T(8,128)S(1)} %get-tuple-element.50), custom_call_target="InvertDiagBlocksLowerTriangular" | custom-call | tf_op jit(solution)/shard_map/jit(cholesky)/cholesky | solution.py:21
  358.6 11.7 %cholesky.147 = f32[128,128]{1,0:T(8,128)S(1)} custom-call(f32[128,128]{1,0:T(8,128)S(1)} %convolution_subtract_fusion.3), custom_call_target="Cholesky" | custom-call | tf_op jit(solution)/shard_map/jit(cholesky)/cholesky | solution.py:21
  372.6 4.1 while.4
  373.2 1.4 bitcast_dynamic-update-slice_fusion.4
  375.3 1.4 bitcast_dynamic-update-slice_fusion.4
  376.7 19.7 %custom-call.14 = f32[2,128,128]{1,2,0:T(8,128)S(1)} custom-call(f32[2,128,128]{2,1,0:T(8,128)S(1)} %get-tuple-element.21), custom_call_target="InvertDiagBlocksLowerTriangular" | custom-call | tf_op jit(solution)/shard_map/triangular_solve/custom-call.0 | solution.py:22
  397.2 1.1 fusion.2
  398.6 140.5 %all-reduce.9.cloned.1.call-done = f32[256,256]{0,1:T(8,128)} async-done(((f32[256,256]{0,1:T(8,128)}), f32[256,256]{0,1:T(8,128)}) %all-reduce.9.cloned.1.call-update) | async-done | bytes 262160 | tf_op jit(solution)/shard_map/psum | solution.py:26
  541.1 11.7 %cholesky.164 = f32[128,128]{1,0:T(8,128)S(1)} custom-call(f32[128,128]{1,0:T(8,128)S(1)} %cholesky.197), custom_call_target="Cholesky" | custom-call | tf_op jit(solution)/shard_map/jit(cholesky)/cholesky | solution.py:21
  553.5 9.8 %custom-call.15 = f32[1,128,128]{1,2,0:T(8,128)S(1)} custom-call(f32[1,128,128]{2,1,0:T(8,128)S(1)} %get-tuple-element.46), custom_call_target="InvertDiagBlocksLowerTriangular" | custom-call | tf_op jit(solution)/shard_map/jit(cholesky)/cholesky | solution.py:21
  563.8 11.7 %cholesky.181 = f32[128,128]{1,0:T(8,128)S(1)} custom-call(f32[128,128]{1,0:T(8,128)S(1)} %convolution_subtract_fusion.1), custom_call_target="Cholesky" | custom-call | tf_op jit(solution)/shard_map/jit(cholesky)/cholesky | solution.py:21
  577.7 4.4 while.5
  578.6 1.4 bitcast_dynamic-update-slice_fusion.5
  580.6 1.4 bitcast_dynamic-update-slice_fusion.5
  582.1 19.7 %custom-call.16 = f32[2,128,128]{1,2,0:T(8,128)S(1)} custom-call(f32[2,128,128]{2,1,0:T(8,128)S(1)} %get-tuple-element.22), custom_call_target="InvertDiagBlocksLowerTriangular" | custom-call | tf_op jit(solution)/shard_map/triangular_solve/custom-call.0 | solution.py:22
  603.3 46.4 %all-gather.2.cloned.1.call-done = f32[4096,256]{0,1:T(8,128)} async-done(((f32[128,256]{0,1:T(8,128)}), f32[4096,256]{0,1:T(8,128)}) %all-gather.2.cloned.1.call-update) | async-done | bytes 4194320 | tf_op jit(solution)/shard_map/all_gather | solution.py:51
  649.7 5.6 copy.8
  (53 shorter events, 14.7 us)
Async XLA Ops:
  6.5 80.7 %all-reduce.5.cloned.1.call-start = ((), (), s32[]{:S(2)}) async-start(), calls=%async_computation.1 | async-start | bytes 4194304 | tf_op jit(solution)/shard_map/psum | solution.py:31
  25.1 160.4 %reduce-scatter.2.cloned.1.call-start = ((), (), s32[]{:S(2)}) async-start(), calls=%async_computation.2 | async-start | bytes 4325376 | tf_op jit(solution)/shard_map/reduce_scatter | solution.py:35
  105.0 229.5 %all-reduce.7.cloned.1.call-start = ((), (), s32[]{:S(2)}) async-start(), calls=%async_computation.3 | async-start | bytes 524288 | tf_op jit(solution)/shard_map/psum | solution.py:26
  187.5 351.5 %all-reduce.9.cloned.1.call-start = ((), (), s32[]{:S(2)}) async-start(), calls=%async_computation.4 | async-start | bytes 524288 | tf_op jit(solution)/shard_map/psum | solution.py:26
  398.3 251.4 %all-gather.2.cloned.1.call-start = ((), (), s32[]{:S(2)}) async-start(), calls=%async_computation.5 | async-start | bytes 4325376 | tf_op jit(solution)/shard_map/all_gather | solution.py:51
Sparse Core Ops, SparseCore 0:
  25.2 61.9 all-reduce.4
  105.1 80.3 reduce-scatter.1
  190.3 144.1 all-reduce.6
  398.4 140.5 all-reduce.8
  603.4 46.2 all-gather.1
where the time goes:
time: 662 us
  waiting for transfers between devices  475 us (72%)
  other arithmetic  112 us (17%)
  matrix products  40.9 us (6%)
  local copies, waits for them, and re-layouts  17 us (3%)
  between operations  16 us (2%)
    psum x2, waiting for transfers between devices, gram_wide(): return lax.psum(gram_of(block), ('item', 'user'))  287 us
    reduce_scatter x1, waiting for transfers between devices, local(): lax.psum_scatter(lax.dot_general(interactions, user_sketch, (((0,), (0,))...  79.4 us
    another operation x13, other arithmetic, factor(): lower = jnp.linalg.cholesky(gram)  68.7 us
    psum x1, waiting for transfers between devices, local(): user_sketch = lax.psum(local_rows, 'item')  62.1 us
    all_gather x1, waiting for transfers between devices, local(): return lax.all_gather(factor_scale * block, 'user', axis=0, tiled=True)  46.4 us
    another operation x5, other arithmetic, factor(): lax.linalg.triangular_solve(lower, block, left_side=False, lower=True, tr...  39.4 us
    dot_general x1, matrix products, local(): jnp.dot(interactions, omega, precision=highest, preferred_element_type=jn...  18.5 us
    dot_general x1, matrix products, local(): lax.dot_general(interactions, user_sketch, (((0,), (0,)), ((), ())), prec...  17.8 us
  transfers between devices with their start and end apart: 5, of which 5 were waited for; matrix products, arithmetic and copies ran while one was open for 0% of the time, Pallas kernels for 0%

commit v1 on v0

--- a/solution.py
+++ b/solution.py
@@ -23,7 +23,7 @@
 
 
 def gram_wide(block):
-    return lax.psum(gram_of(block), ("item", "user"))
+    return jnp.sum(lax.all_gather(gram_of(block), ("item", "user")), axis=0)
 
 
 def local(interactions, omega):

time: 662 us -> 611 us (0.923)
  waiting for transfers between devices: 475 us -> 404 us
  other arithmetic: 112 us -> 134 us
    psum x2 -> x0, waiting for transfers between devices: 287 us -> none  [gram_wide(): return lax.psum(gram_of(block), ('item', 'user'))]
    all_gather x0 -> x2, waiting for transfers between devices: none -> 214 us  [gram_wide(): return jnp.sum(lax.all_gather(gram_of(block), ('item', 'user')), axis=0)]
    reduce_sum x0 -> x2, other arithmetic: none -> 24 us  [gram_wide(): return jnp.sum(lax.all_gather(gram_of(block), ('item', 'user')), axis=0)]
where the time goes in v1:
time: 611 us
  waiting for transfers between devices  404 us (66%)
  other arithmetic  134 us (22%)
  matrix products  40.9 us (7%)
  between operations  16.1 us (3%)
  local copies, waits for them, and re-layouts  15.1 us (2%)
    all_gather x2, waiting for transfers between devices, gram_wide(): return jnp.sum(lax.all_gather(gram_of(block), ('item', 'user')), axis=0)  214 us
    reduce_scatter x1, waiting for transfers between devices, local(): lax.psum_scatter(lax.dot_general(interactions, user_sketch, (((0,), (0,))...  79.4 us
    another operation x13, other arithmetic, factor(): lower = jnp.linalg.cholesky(gram)  68.7 us
    psum x1, waiting for transfers between devices, local(): user_sketch = lax.psum(local_rows, 'item')  62.1 us
    all_gather x1, waiting for transfers between devices, local(): return lax.all_gather(factor_scale * block, 'user', axis=0, tiled=True)  47.9 us
    another operation x5, other arithmetic, factor(): lax.linalg.triangular_solve(lower, block, left_side=False, lower=True, tr...  39.9 us
    reduce_sum x2, other arithmetic, gram_wide(): return jnp.sum(lax.all_gather(gram_of(block), ('item', 'user')), axis=0)  24 us
    dot_general x1, matrix products, local(): jnp.dot(interactions, omega, precision=highest, preferred_element_type=jn...  18.5 us
  transfers between devices with their start and end apart: 5, of which 5 were waited for; matrix products, arithmetic and copies ran while one was open for 0% of the time, Pallas kernels for 0%

profile of v1, /device:TPU:1, one launch (start us, length us, event | category | flops | bytes accessed | tf_op | source)
XLA Modules:
  0.0 610.6 jit_solution(2706185334762135721)
XLA Ops:
  6.5 18.5 %fusion.27 = f32[2048,256]{1,0:T(8,128)} fusion(bf16[2048,4096]{1,0:T(8,128)(2,1)} %param.5, f32[4096,256]{1,0:T(8,128)} %param.6), kind=kOutput, calls=%fused_computation.63 | convolution fusion | flops 25769803776 | bytes 23068672 | tf_op jit(solution)/shard_map/dot_general | solution.py:30
  25.1 62.1 %all-reduce.3.cloned.1.call-done = f32[2048,256]{1,0:T(8,128)} async-done(((f32[2048,256]{1,0:T(8,128)}), f32[2048,256]{1,0:T(8,128)}) %all-reduce.3.cloned.1.call-update) | async-done | bytes 2097168 | tf_op jit(solution)/shard_map/psum | solution.py:31
  87.2 17.8 %convolution_bitcast_fusion = f32[4096,256]{0,1:T(8,128)} fusion(f32[2048,256]{1,0:T(8,128)} %all-reduce.3.cloned.1.call-done, bf16[2048,4096]{1,0:T(8,128)(2,1)} %param.5), kind=kOutput, calls=%fused_computation.4 | convolution fusion | flops 25769803776 | bytes 23068672 | tf_op jit(solution)/shard_map/dot_general | solution.py:36
  106.1 79.4 %reduce-scatter.2.cloned.1.call-done = f32[128,256]{0,1:T(8,128)} async-done(((f32[4096,256]{0,1:T(8,128)}), f32[128,256]{0,1:T(8,128)}) %reduce-scatter.2.cloned.1.call-update) | async-done | bytes 131088 | tf_op jit(solution)/shard_map/reduce_scatter | solution.py:35
  187.8 108.5 %all-gather.8.cloned.1.call-done = f32[32768,256]{1,0:T(8,128)} async-done(((f32[256,256]{1,0:T(8,128)}), f32[32768,256]{1,0:T(8,128)}) %all-gather.8.cloned.1.call-update) | async-done | bytes 33554448 | tf_op jit(solution)/shard_map/all_gather | solution.py:26
  296.3 12.0 %reduce_sum.18 = f32[256,256]{1,0:T(8,128)S(1)} reduce(f32[128,256,256]{2,1,0:T(8,128)} %bitcast.76, f32[]{:T(128)} %constant.69.clone.1), dimensions={0}, to_apply=%region_2.0 | reduce | flops 8323072 | bytes 33816580 | tf_op jit(solution)/shard_map/reduce_sum | solution.py:26
  308.5 11.7 %cholesky.130 = f32[128,128]{1,0:T(8,128)S(1)} custom-call(f32[128,128]{1,0:T(8,128)S(1)} %cholesky.194), custom_call_target="Cholesky" | custom-call | tf_op jit(solution)/shard_map/jit(cholesky)/cholesky | solution.py:21
  320.2 9.8 %custom-call.13 = f32[1,128,128]{1,2,0:T(8,128)S(1)} custom-call(f32[1,128,128]{2,1,0:T(8,128)S(1)} %get-tuple-element.50), custom_call_target="InvertDiagBlocksLowerTriangular" | custom-call | tf_op jit(solution)/shard_map/jit(cholesky)/cholesky | solution.py:21
  330.6 11.7 %cholesky.147 = f32[128,128]{1,0:T(8,128)S(1)} custom-call(f32[128,128]{1,0:T(8,128)S(1)} %convolution_subtract_fusion.3), custom_call_target="Cholesky" | custom-call | tf_op jit(solution)/shard_map/jit(cholesky)/cholesky | solution.py:21
  344.5 4.1 while.4
  345.1 1.4 bitcast_dynamic-update-slice_fusion.4
  347.2 1.4 bitcast_dynamic-update-slice_fusion.4
  348.6 19.9 %custom-call.14 = f32[2,128,128]{1,2,0:T(8,128)S(1)} custom-call(f32[2,128,128]{2,1,0:T(8,128)S(1)} %get-tuple-element.21), custom_call_target="InvertDiagBlocksLowerTriangular" | custom-call | tf_op jit(solution)/shard_map/triangular_solve/custom-call.0 | solution.py:22
  370.5 105.8 %all-gather.10.cloned.1.call-done = f32[32768,256]{1,0:T(8,128)} async-done(((f32[256,256]{1,0:T(8,128)}), f32[32768,256]{1,0:T(8,128)}) %all-gather.10.cloned.1.call-update) | async-done | bytes 33554448 | tf_op jit(solution)/shard_map/all_gather | solution.py:26
  476.3 12.0 %reduce_sum.19 = f32[256,256]{1,0:T(8,128)S(1)} reduce(f32[128,256,256]{2,1,0:T(8,128)} %bitcast.77, f32[]{:T(128)} %constant.69.clone.1), dimensions={0}, to_apply=%region_7.10 | reduce | flops 8323072 | bytes 33816580 | tf_op jit(solution)/shard_map/reduce_sum | solution.py:26
  488.4 11.7 %cholesky.164 = f32[128,128]{1,0:T(8,128)S(1)} custom-call(f32[128,128]{1,0:T(8,128)S(1)} %cholesky.197), custom_call_target="Cholesky" | custom-call | tf_op jit(solution)/shard_map/jit(cholesky)/cholesky | solution.py:21
  500.2 9.8 %custom-call.15 = f32[1,128,128]{1,2,0:T(8,128)S(1)} custom-call(f32[1,128,128]{2,1,0:T(8,128)S(1)} %get-tuple-element.46), custom_call_target="InvertDiagBlocksLowerTriangular" | custom-call | tf_op jit(solution)/shard_map/jit(cholesky)/cholesky | solution.py:21
  510.5 11.7 %cholesky.181 = f32[128,128]{1,0:T(8,128)S(1)} custom-call(f32[128,128]{1,0:T(8,128)S(1)} %convolution_subtract_fusion.1), custom_call_target="Cholesky" | custom-call | tf_op jit(solution)/shard_map/jit(cholesky)/cholesky | solution.py:21
  525.0 4.1 while.5
  525.6 1.4 bitcast_dynamic-update-slice_fusion.5
  527.7 1.4 bitcast_dynamic-update-slice_fusion.5
  529.1 19.9 %custom-call.16 = f32[2,128,128]{1,2,0:T(8,128)S(1)} custom-call(f32[2,128,128]{2,1,0:T(8,128)S(1)} %get-tuple-element.22), custom_call_target="InvertDiagBlocksLowerTriangular" | custom-call | tf_op jit(solution)/shard_map/triangular_solve/custom-call.0 | solution.py:22
  550.5 47.9 %all-gather.6.cloned.1.call-done = f32[4096,256]{0,1:T(8,128)} async-done(((f32[128,256]{0,1:T(8,128)}), f32[4096,256]{0,1:T(8,128)}) %all-gather.6.cloned.1.call-update) | async-done | bytes 4194320 | tf_op jit(solution)/shard_map/all_gather | solution.py:51
  598.5 5.6 copy.10
  (55 shorter events, 12.8 us)
Async XLA Ops:
  6.5 80.7 %all-reduce.3.cloned.1.call-start = ((), (), s32[]{:S(2)}) async-start(), calls=%async_computation.1 | async-start | bytes 4194304 | tf_op jit(solution)/shard_map/psum | solution.py:31
  25.1 160.4 %reduce-scatter.2.cloned.1.call-start = ((), (), s32[]{:S(2)}) async-start(), calls=%async_computation.2 | async-start | bytes 4325376 | tf_op jit(solution)/shard_map/reduce_scatter | solution.py:35
  105.0 191.3 %all-gather.8.cloned.1.call-start = ((), (), s32[]{:S(2)}) async-start(), calls=%async_computation.4 | async-start | bytes 33816576 | tf_op jit(solution)/shard_map/all_gather | solution.py:26
  187.5 288.7 %all-gather.10.cloned.1.call-start = ((), (), s32[]{:S(2)}) async-start(), calls=%async_computation.5 | async-start | bytes 33816576 | tf_op jit(solution)/shard_map/all_gather | solution.py:26
  370.4 228.0 %all-gather.6.cloned.1.call-start = ((), (), s32[]{:S(2)}) async-start(), calls=%async_computation.3 | async-start | bytes 4325376 | tf_op jit(solution)/shard_map/all_gather | solution.py:51
Sparse Core Ops, SparseCore 0:
  25.2 61.9 all-reduce.2
  105.1 80.3 reduce-scatter.1
  188.5 107.7 all-gather.7
  370.6 105.6 all-gather.9
  550.7 47.7 all-gather.5
